TPU v7x, 128 devices: a whole 4x4x4 slice. The times are simulated.
128 devices in a mesh: box: 32 (over x, z, core), dir: 4 (over y).
Axes of the slice: x: 4, y: 4, z: 4, core: 2. Of those that a mesh axis runs over, the one named last changes fastest.
Arguments:
- child_pat: bfloat16 [4096, 2, 8, 2048], P('box', None, None, 'dir'), may hold values from -6 to 6
- interp: bfloat16 [64, 4, 128, 128], P('dir'), may hold values from -0.25 to 0.25
- interp_blocks: int32 [64, 4], P('dir'), may hold values from 0 to 15, as said below
- shift_angle: float32 [8, 8192], P(None, 'dir'), may hold values from -3.140625 to 3.140625
- slot_parent: int32 [512], replicated, may hold values from 0 to 511, each once
- far_list: int32 [512, 189], replicated, may hold values from -1 to 511, as said below
- trans: float32 [2, 343, 8192], P(None, None, 'dir'), may hold values from -0.15625 to 0.15625
Outputs:
- far_field: float32 [512, 2, 8, 8192], P('box', None, None, 'dir')
Inputs may be any that keep to these rules, and one draw needn't show every extreme that they name: `interp_blocks`: entry (j, b) is (j * 16 // 64 + o) modulo 16, for four different o of -2 to 2 in increasing order. `far_list`: row p lists, in increasing order of code(p, q), the occupied parents q whose own parents are neighbours of p's parent (coordinates differ by at most one) and that are not neighbours of p, then -1 to the end; each coordinate of q - p lies within -3 to 3; some row lists 189 partners.
All inputs are finite; a program needn't handle non-finite values.
Results may differ from a plain program's by a relative error of at most 0.0029.
Values may be sent and summed in bfloat16 or wider, within the bound.
A program may use at most 192 MiB of HBM per device.

v0:
```python
import jax
import jax.numpy as jnp
from jax import lax
from jax.experimental import pallas as pl
from jax.experimental.pallas import tpu as pltpu
from jax.sharding import PartitionSpec as P

G = 8
F1 = 18
NF = F1 * F1


def toom_in(v):
    a, b = v[0] + v[2], v[1] + v[3]
    c, d = v[0] + 4.0 * v[2], 2.0 * v[1] + 8.0 * v[3]
    return [v[0], v[3], a + b, a - b, c + d, c - d]


def line_in(x):
    even, odd = x[0::2], x[1::2]
    both = [e + o for e, o in zip(even, odd)]
    return toom_in(both) + toom_in(odd) + toom_in(even)


def toom_kernel(k):
    h2, h1, h0 = k
    a, b = (h0 + h2) * 0.5, h1 * 0.5
    c, d = (h0 + 4.0 * h2) * (1.0 / 24.0), h1 * (1.0 / 12.0)
    return [h0, h2, a + b, a - b, c + d, c - d]


def line_kernel(t):
    k0 = [t[1], t[3], t[5]]
    up = [t[2] - t[1], t[4] - t[3], t[6] - t[5]]
    down = [t[0] - t[1], t[2] - t[3], t[4] - t[5]]
    return toom_kernel(k0) + toom_kernel(up) + toom_kernel(down)


def toom_out(m):
    z0, z5 = m[0], m[1]
    e1, o1 = m[2] + m[3], m[2] - m[3]
    e2, d2 = m[4] + m[5], m[4] - m[5]
    z4 = e2 - e1 * (1.0 / 3.0) + z0 * 0.25
    z2 = e1 - z0 - z4
    z3 = 2.0 * d2 - o1 * (1.0 / 3.0) - 5.0 * z5
    z1 = o1 - z3 - z5
    return [z1, z2, z3, z4]


def line_out(m):
    base, up, down = toom_out(m[0:6]), toom_out(m[6:12]), toom_out(m[12:18])
    out = []
    for i in range(4):
        out += [base[i] + up[i], base[i] + down[i]]
    return out


def upsample_kernel(rel, before, own, after, interp, cosine, sine, out, weight, total):
    slots = before.shape[0] // 128

    @pl.when(pl.program_id(0) == 0)
    def _():
        weight[...] = jnp.zeros_like(weight)
        for j in range(16):
            for b in range(4):
                start = pl.multiple_of(rel[j * 4 + b] * 128, 128)
                weight[j // 4, pl.ds(start, 128), pl.ds((j % 4) * 128, 128)] = interp[j, b]

    row = lax.broadcasted_iota(jnp.int32, (8, 128), 0)
    low = row < 4
    for c in range(4):
        parts = []
        first, last = c, c + 5
        if first < 2:
            parts.append((before, first * 128, (2 - first) * 128, 0))
        lo, hi = max(first, 2), min(last, 6)
        parts.append((own, (lo - 2) * 128, (hi - lo) * 128, (lo - first) * 128))
        if last > 6:
            parts.append((after, 0, (last - 6) * 128, (6 - first) * 128))
        acc = None
        for ref, col, width, at in parts:
            piece = jnp.dot(
                ref[:, pl.ds(col, width)],
                weight[c, pl.ds(at, width), :],
                preferred_element_type=jnp.float32,
            )
            acc = piece if acc is None else acc + piece
        total[...] = acc

        def one(step, carry, c=c):
            pair = step // 4
            tile = step % 4
            lane = pl.multiple_of(tile * 128, 128)
            wide = pl.multiple_of(c * 512 + tile * 128, 128)
            halves = [[], []]
            for k in range(2):
                re = jnp.zeros((8, 128), jnp.float32)
                im = jnp.zeros((8, 128), jnp.float32)
                for h in range(8):
                    base = pl.multiple_of((pair * 2 + k) * 128 + h * 16, 16)
                    ur = total[pl.ds(base, 8), pl.ds(lane, 128)]
                    ui = total[pl.ds(base + 8, 8), pl.ds(lane, 128)]
                    cs = jnp.broadcast_to(cosine[h : h + 1, pl.ds(wide, 128)], (8, 128))
                    sn = jnp.broadcast_to(sine[h : h + 1, pl.ds(wide, 128)], (8, 128))
                    re = re + (cs * ur - sn * ui)
                    im = im + (sn * ur + cs * ui)
                halves[0].append(jnp.where(low, re, pltpu.roll(im, 4, 0)))
                halves[1].append(jnp.where(low, pltpu.roll(re, 4, 0), im))
            rows = pl.ds(pl.multiple_of(pair * 16, 16), 16)
            for k in range(2):
                value = jnp.concatenate(halves[k], axis=0).astype(jnp.bfloat16)
                out[(c * 4 + tile) * 2 + k, rows, :] = value
            return carry

        lax.fori_loop(0, (slots // 2) * 4, one, 0)


def upsample(before, own, after, interp, rel, cosine, sine):
    rows = own.shape[0]
    chunk = 512
    grid_spec = pltpu.PrefetchScalarGridSpec(
        num_scalar_prefetch=1,
        grid=(rows // chunk,),
        in_specs=[
            pl.BlockSpec((chunk, 256), lambda i, r: (i, 0)),
            pl.BlockSpec((chunk, 512), lambda i, r: (i, 0)),
            pl.BlockSpec((chunk, 256), lambda i, r: (i, 0)),
            pl.BlockSpec((16, 4, 128, 128), lambda i, r: (0, 0, 0, 0)),
            pl.BlockSpec((8, 2048), lambda i, r: (0, 0)),
            pl.BlockSpec((8, 2048), lambda i, r: (0, 0)),
        ],
        out_specs=pl.BlockSpec((32, chunk // 16, 128), lambda i, r: (0, i, 0)),
        scratch_shapes=[
            pltpu.VMEM((4, 640, 512), jnp.bfloat16),
            pltpu.VMEM((chunk, 512), jnp.float32),
        ],
    )
    return pl.pallas_call(
        upsample_kernel,
        grid_spec=grid_spec,
        out_shape=jax.ShapeDtypeStruct((32, rows // 16, 128), jnp.bfloat16),
    )(rel, before, own, after, interp, cosine, sine)


def translate_kernel(chunk_id, slot_parent, occupied, pats, table, out, grid_x, lines, spec, tab_z, tab):
    row = lax.broadcasted_iota(jnp.int32, (8, 128), 0)
    sign = jnp.where(row < 4, -1.0, 1.0).astype(jnp.float32)
    row7 = lax.broadcasted_iota(jnp.int32, (7, 128), 0)
    far_x = (row7 < 2) | (row7 > 4)

    def place(i, carry):
        both = pats[pl.ds(pl.multiple_of(i * 16, 16), 16), :].astype(jnp.float32)
        for k in range(2):
            p = slot_parent[2 * i + k]
            grid_x[p] = both[8 * k : 8 * k + 8] * occupied[p]
        return carry

    lax.fori_loop(0, 256, place, 0, unroll=4)

    for part in range(2):
        for y in range(7):
            vals = []
            for z in range(7):
                t = table[part, pl.ds(y * 7 + z, 7, stride=49), :]
                if 2 <= y <= 4 and 2 <= z <= 4:
                    t = jnp.where(far_x, t, 0.0)
                vals.append(t)
            for f, v in enumerate(line_kernel(vals)):
                tab_z[(part * 7 + y) * F1 + f, 0:7, :] = v

    def table_y(i, carry):
        part, fz = i // F1, i % F1
        vals = line_kernel([tab_z[(part * 7 + y) * F1 + fz] for y in range(7)])
        for fy, v in enumerate(vals):
            tab[part, fy * F1 + fz] = v
        return carry

    lax.fori_loop(0, 2 * F1, table_y, 0)

    def in_z(i, carry):
        for f, v in enumerate(line_in([grid_x[i * 8 + z] for z in range(8)])):
            lines[i * F1 + f] = v
        return carry

    lax.fori_loop(0, 64, in_z, 0)

    def in_y(i, carry):
        x, fz = i // F1, i % F1
        vals = line_in([lines[(x * 8 + y) * F1 + fz] for y in range(8)])
        for fy, v in enumerate(vals):
            spec[fy * F1 + fz, x] = v
        return carry

    lax.fori_loop(0, 8 * F1, in_y, 0)

    def product(f, carry):
        src = [spec[f, q] for q in range(8)]
        direct, cross = [None] * 8, [None] * 8
        for d in range(-3, 4):
            a = jnp.broadcast_to(tab[0, f, d + 3 : d + 4, :], (8, 128))
            b = jnp.broadcast_to(tab[1, f, d + 3 : d + 4, :], (8, 128))
            for p in range(8):
                q = p + d
                if q < 0 or q > 7 or abs(q // 2 - p // 2) > 1:
                    continue
                u, w = a * src[q], b * src[q]
                direct[p] = u if direct[p] is None else direct[p] + u
                cross[p] = w if cross[p] is None else cross[p] + w
        for p in range(8):
            spec[f, p] = direct[p] + sign * pltpu.roll(cross[p], 4, 0)
        return carry

    lax.fori_loop(0, NF, product, 0, unroll=2)

    def out_y(i, carry):
        x, fz = i // F1, i % F1
        vals = line_out([spec[fy * F1 + fz, x] for fy in range(F1)])
        for y, v in enumerate(vals):
            lines[(x * 8 + y) * F1 + fz] = v
        return carry

    lax.fori_loop(0, 8 * F1, out_y, 0)

    def out_z(i, carry):
        for z, v in enumerate(line_out([lines[i * F1 + f] for f in range(F1)])):
            grid_x[i * 8 + z] = v
        return carry

    lax.fori_loop(0, 64, out_z, 0)

    def give(i, carry):
        vals = [grid_x[slot_parent[2 * i + k]] for k in range(2)]
        both = jnp.concatenate(vals, axis=0).astype(out.dtype)
        out[pl.ds(pl.multiple_of(i * 16, 16), 16), :] = both
        return carry

    lax.fori_loop(0, 256, give, 0, unroll=4)


def translate(pats, table, chunk_id, slot_parent, occupied):
    grid_spec = pltpu.PrefetchScalarGridSpec(
        num_scalar_prefetch=3,
        grid=(1,),
        in_specs=[
            pl.BlockSpec((4096, 128), lambda i, c, s, o: (0, 0)),
            pl.BlockSpec((2, 343, 128), lambda i, c, s, o: (0, 0, c[0])),
        ],
        out_specs=pl.BlockSpec((4096, 128), lambda i, c, s, o: (0, 0)),
        scratch_shapes=[
            pltpu.VMEM((512, 8, 128), jnp.float32),
            pltpu.VMEM((64 * F1, 8, 128), jnp.float32),
            pltpu.VMEM((NF, 8, 8, 128), jnp.float32),
            pltpu.VMEM((14 * F1, 8, 128), jnp.float32),
            pltpu.VMEM((2, NF, 8, 128), jnp.float32),
        ],
    )
    return pl.pallas_call(
        translate_kernel,
        grid_spec=grid_spec,
        out_shape=jax.ShapeDtypeStruct((4096, 128), jnp.bfloat16),
    )(chunk_id, slot_parent, occupied, pats, table)


def arrange_kernel(got, out):
    low = lax.broadcasted_iota(jnp.int32, (8, 128), 0) < 4
    for pair in range(got.shape[1] // 16):
        for c in range(16):
            first = got[2 * c, pair * 16 : pair * 16 + 16, :].astype(jnp.float32)
            second = got[2 * c + 1, pair * 16 : pair * 16 + 16, :].astype(jnp.float32)
            for k in range(2):
                h0, h1 = first[8 * k : 8 * k + 8], second[8 * k : 8 * k + 8]
                s = pair * 2 + k
                out[s, 0, :, c * 128 : c * 128 + 128] = jnp.where(low, h0, pltpu.roll(h1, 4, 0))
                out[s, 1, :, c * 128 : c * 128 + 128] = jnp.where(low, pltpu.roll(h0, 4, 0), h1)


def arrange(got):
    return pl.pallas_call(
        arrange_kernel,
        grid=(4,),
        in_specs=[pl.BlockSpec((32, 32, 128), lambda i: (0, i, 0))],
        out_specs=pl.BlockSpec((4, 2, 8, 2048), lambda i: (i, 0, 0, 0)),
        out_shape=jax.ShapeDtypeStruct((16, 2, 8, 2048), jnp.float32),
    )(got)


def shards(child_pat, interp, interp_blocks, shift_angle, slot_parent, far_list, trans):
    dirs = lax.axis_size("dir")
    up = [(i, (i + 1) % dirs) for i in range(dirs)]
    down = [(j, i) for i, j in up]
    flat = child_pat.reshape(2048, 512)
    before = lax.ppermute(flat[:, 256:], "dir", up)
    after = lax.ppermute(flat[:, :256], "dir", down)
    centre = lax.axis_index("dir") * 4 + jnp.arange(16, dtype=jnp.int32)[:, None] // 4
    rel = ((interp_blocks - centre + 2) % 16).reshape(64)
    pieces = upsample(before, flat, after, interp, rel, jnp.cos(shift_angle), jnp.sin(shift_angle))
    pats = lax.all_to_all(pieces, "box", 0, 0, tiled=True).reshape(4096, 128)
    ident = jnp.arange(512, dtype=jnp.int32)[:, None]
    watch = jnp.concatenate([far_list[128:], far_list[256:384]], axis=0)
    occupied = jnp.any(watch == ident, axis=1).astype(jnp.float32)
    chunk_id = (lax.axis_index("box") // 2).astype(jnp.int32).reshape(1)
    local = translate(pats, trans, chunk_id, slot_parent, occupied)
    back = lax.all_to_all(local.reshape(32, 128, 128), "box", 0, 0, tiled=True)
    return arrange(back)


def solution(mesh):
    in_specs = (
        P("box", None, None, "dir"),
        P("dir", None, None, None),
        P("dir", None),
        P(None, "dir"),
        P(),
        P(),
        P(None, None, "dir"),
    )
    out_specs = P("box", None, None, "dir")
    return jax.shard_map(shards, mesh=mesh, in_specs=in_specs, out_specs=out_specs, check_vma=False)
```

profile of v0, /device:TPU:1, one launch (start us, length us, event | category | flops | bytes accessed | tf_op | source)
XLA Modules:
  0.0 128.5 jit_solution(18267299210318129776)
XLA Ops:
  0.0 0.0 copy-start.3
  0.0 0.0 copy-start.2
  0.0 1.7 %fusion.3 = (bf16[2048,256]{1,0:T(8,128)(2,1)S(1)}, bf16[2048,256]{1,0:T(8,128)(2,1)S(1)}) fusion(bf16[2048,512]{1,0:T(8,128)(2,1)} %bitcast.4), kind=kLoop, calls=%fused_computation.11 | loop fusion | bytes 4194304 | tf_op jit(solution)/shard_map/slice | solution.py:293
  1.7 3.6 %collective-permute-start.1 = (bf16[2048,256]{1,0:T(8,128)(2,1)S(1)}, bf16[2048,256]{1,0:T(8,128)(2,1)S(1)}, u32[]{:S(2)}, u32[]{:S(2)}) collective-permute-start(bf16[2048,256]{1,0:T(8,128)(2,1)S(1)} %get-tuple-element.5), channel_id=1, source_target_pairs={{1,0},{2,1},{3,2},{0,3},{5,4},{6,5},{7,6},{4,7},{9,8},{10,9},{11,1... | collective-permute-start | bytes 3145736 | tf_op jit(solution)/shard_map/ppermute | solution.py:293
  5.3 0.0 collective-permute-start
  5.3 0.0 copy-done.3
  5.4 0.1 copy.10
  5.5 0.6 reshape.55.rel
  6.1 0.0 copy-done.2
  6.1 0.9 fusion.4
  7.0 20.2 %collective-permute-done.1.after = bf16[2048,256]{1,0:T(8,128)(2,1)S(1)} collective-permute-done((bf16[2048,256]{1,0:T(8,128)(2,1)S(1)}, bf16[2048,256]{1,0:T(8,128)(2,1)S(1)}, u32[]{:S(2)}, u32[]{:S(2)}) %collective-permute-start.1) | collective-permute-done | bytes 1048608 | tf_op jit(solution)/shard_map/ppermute | solution.py:293
  27.2 0.0 copy-start.1
  27.2 3.2 %collective-permute-done.before = bf16[2048,256]{1,0:T(8,128)(2,1)} collective-permute-done((bf16[2048,256]{1,0:T(8,128)(2,1)S(1)}, bf16[2048,256]{1,0:T(8,128)(2,1)}, u32[]{:S(2)}, u32[]{:S(2)}) %collective-permute-start) | collective-permute-done | bytes 1048608 | tf_op jit(solution)/shard_map/ppermute | solution.py:292
  30.4 0.0 copy-done.1
  30.4 21.8 %shard_map.73 = bf16[32,128,128]{2,1,0:T(8,128)(2,1)} custom-call(s32[64]{0:T(128)} %reshape.55.rel, bf16[2048,256]{1,0:T(8,128)(2,1)} %collective-permute-done.before, bf16[2048,512]{1,0:T(8,128)(2,1)} %bitcast.5, bf16[2048,256]{1,0:T(8,128)(2,1)} %copy-done.1, bf16[16,4,128,128]{3,2,1,0:T(8,128)(2,1)} %interp.1, f32[8,2048]{1,0:T(8,128)} %get-tuple-element.8.cosine, ...), custom_call_target="tpu_custom_call" | custom-call | tf_op jit(solution)/shard_map/pallas_call | solution.py:138
  52.2 0.0 slice-start
  52.2 0.0 slice-start.1
  52.2 9.9 %all-to-all-start = ((bf16[32,128,128]{2,1,0:T(8,128)(2,1)}), bf16[32,128,128]{2,1,0:T(8,128)(2,1)S(1)}, u32[]{:S(2)}, u32[]{:S(2)}) async-start(bf16[32,128,128]{2,1,0:T(8,128)(2,1)} %shard_map.73), calls=%async_computation | async-start | bytes 2097152 | tf_op jit(solution)/shard_map/all_to_all | solution.py:297
  62.1 0.0 slice-done
  62.1 0.0 slice-done.1
  62.1 0.1 fusion
  62.2 0.6 convert_element_type.3.occupied
  62.8 8.3 %copy.11.table = f32[2,343,2048]{2,1,0:T(8,128)} copy(f32[2,343,2048]{2,0,1:T(2,128)} %param.13) | data formatting | bytes 11239424 | tf_op args[6]
  71.1 7.9 %all-to-all-done = bf16[32,128,128]{2,1,0:T(8,128)(2,1)S(1)} async-done(((bf16[32,128,128]{2,1,0:T(8,128)(2,1)}), bf16[32,128,128]{2,1,0:T(8,128)(2,1)S(1)}, u32[]{:S(2)}, u32[]{:S(2)}) %all-to-all-start) | async-done | bytes 1048608 | tf_op jit(solution)/shard_map/all_to_all | solution.py:297
  79.0 0.0 copy-start
  79.0 1.0 copy-done
  80.0 23.5 %shard_map.74 = bf16[4096,128]{1,0:T(8,128)(2,1)} custom-call(s32[1]{0:T(128)} %bitcast.chunk_id, s32[512]{0:T(512)} %slot_parent.1, f32[512]{0:T(512)} %convert_element_type.3.occupied, bf16[4096,128]{1,0:T(8,128)(2,1)} %bitcast.6, f32[2,343,2048]{2,1,0:T(8,128)} %copy.11.table), custom_call_target="tpu_custom_call" | custom-call | tf_op jit(solution)/shard_map/pallas_call | solution.py:257
  103.5 21.4 %all_to_all.10.got = bf16[32,128,128]{2,1,0:T(8,128)(2,1)} all-to-all(bf16[32,128,128]{2,1,0:T(8,128)(2,1)} %bitcast.7), channel_id=1, replica_groups=mesh['box'=32,'dir'=4] {'box'}, dimensions={0} | all-to-all | bytes 2097152 | tf_op jit(solution)/shard_map/all_to_all | solution.py:303
  124.9 3.6 %shard_map.75 = f32[16,2,8,2048]{3,2,1,0:T(8,128)} custom-call(bf16[32,128,128]{2,1,0:T(8,128)(2,1)} %all_to_all.10.got), custom_call_target="tpu_custom_call" | custom-call | tf_op jit(solution)/shard_map/pallas_call | solution.py:278
  (2 shorter events, 0.0 us)
Async XLA Ops:
  0.0 5.3 %copy-start.3 = (s32[16,4]{0,1:T(4,128)S(1)}, s32[16,4]{0,1:T(4,128)}, u32[]{:S(2)}) copy-start(s32[16,4]{0,1:T(4,128)} %param.9) | copy-start | bytes 772
  0.0 6.1 %copy-start.2 = (f32[8,2048]{1,0:T(8,128)S(1)}, f32[8,2048]{1,0:T(8,128)}, u32[]{:S(2)}) copy-start(f32[8,2048]{1,0:T(8,128)} %param.10) | copy-start | bytes 196612
  1.7 25.5 %collective-permute-start.1 = (bf16[2048,256]{1,0:T(8,128)(2,1)S(1)}, bf16[2048,256]{1,0:T(8,128)(2,1)S(1)}, u32[]{:S(2)}, u32[]{:S(2)}) collective-permute-start(bf16[2048,256]{1,0:T(8,128)(2,1)S(1)} %get-tuple-element.5), channel_id=1, source_target_pairs={{1,0},{2,1},{3,2},{0,3},{5,4},{6,5},{7,6},{4,7},{9,8},{10,9},{11,1... | collective-permute-start | bytes 3145736 | tf_op jit(solution)/shard_map/ppermute | solution.py:293
  5.3 25.1 %collective-permute-start = (bf16[2048,256]{1,0:T(8,128)(2,1)S(1)}, bf16[2048,256]{1,0:T(8,128)(2,1)}, u32[]{:S(2)}, u32[]{:S(2)}) collective-permute-start(bf16[2048,256]{1,0:T(8,128)(2,1)S(1)} %get-tuple-element.6), channel_id=1, source_target_pairs={{0,1},{1,2},{2,3},{3,0},{4,5},{5,6},{6,7},{7,4},{8,9},{9,10},{10,1... | collective-permute-start | bytes 3145736 | tf_op jit(solution)/shard_map/ppermute | solution.py:292
  27.2 3.2 %copy-start.1 = (bf16[2048,256]{1,0:T(8,128)(2,1)}, bf16[2048,256]{1,0:T(8,128)(2,1)S(1)}, u32[]{:S(2)}) copy-start(bf16[2048,256]{1,0:T(8,128)(2,1)S(1)} %collective-permute-done.1.after) | copy-start | bytes 3145732
  52.2 9.9 %slice-start = ((s32[512,189]{0,1:T(8,128)}), s32[128,189]{0,1:T(8,128)S(1)}, s32[]{:S(2)}) async-start(s32[512,189]{0,1:T(8,128)} %param.12), calls=%async_computation.2 | async-start | bytes 196608 | tf_op jit(solution)/shard_map/slice | solution.py:299
  52.2 9.9 %slice-start.1 = ((s32[512,189]{0,1:T(8,128)}), s32[384,189]{0,1:T(8,128)S(1)}, s32[]{:S(2)}) async-start(s32[512,189]{0,1:T(8,128)} %param.12), calls=%async_computation.3 | async-start | bytes 589824 | tf_op jit(solution)/shard_map/slice | solution.py:299
  52.2 26.8 %all-to-all-start = ((bf16[32,128,128]{2,1,0:T(8,128)(2,1)}), bf16[32,128,128]{2,1,0:T(8,128)(2,1)S(1)}, u32[]{:S(2)}, u32[]{:S(2)}) async-start(bf16[32,128,128]{2,1,0:T(8,128)(2,1)} %shard_map.73), calls=%async_computation | async-start | bytes 2097152 | tf_op jit(solution)/shard_map/all_to_all | solution.py:297
  79.0 1.0 copy-start
where the time goes:
time: 129 us; the launch traced here: 128 us
  Pallas kernels  48.9 us (38%)
  waiting for transfers between devices  31.4 us (24%)
  blocking collectives  21.4 us (17%)
  starting transfers between devices  13.5 us (10%)
  local copies, waits for them, and re-layouts  12.6 us (10%)
    pallas_call x1, Pallas kernels, translate(): pl.pallas_call(translate_kernel, grid_spec=grid_spec, out_shape=jax.Shape...  23.5 us
    pallas_call x1, Pallas kernels, upsample(): pl.pallas_call(upsample_kernel, grid_spec=grid_spec, out_shape=jax.ShapeD...  21.8 us
    all_to_all x1, blocking collectives, shards(): back = lax.all_to_all(local.reshape(32, 128, 128), 'box', 0, 0, tiled=True)  21.4 us
    ppermute x1, waiting for transfers between devices, shards(): after = lax.ppermute(flat[:, :256], 'dir', down)  20.2 us
    all_to_all x1, starting transfers between devices, shards(): pats = lax.all_to_all(pieces, 'box', 0, 0, tiled=True).reshape(4096, 128)  9.88 us
    unnamed x9, local copies, waits for them, and re-layouts  9.28 us
    all_to_all x1, waiting for transfers between devices, shards(): pats = lax.all_to_all(pieces, 'box', 0, 0, tiled=True).reshape(4096, 128)  7.93 us
    ppermute x1, starting transfers between devices, shards(): after = lax.ppermute(flat[:, :256], 'dir', down)  3.62 us
  transfers between devices with their start and end apart: 3, of which 3 were waited for; matrix products, arithmetic and copies ran while one was open for 8% of the time, Pallas kernels for 0%

commit v1 on v0

v1 whole, which is shorter than its diff:
```python
import jax
import jax.numpy as jnp
from jax import lax
from jax.experimental import pallas as pl
from jax.experimental.pallas import tpu as pltpu
from jax.sharding import PartitionSpec as P

G = 8
F1 = 18
NF = F1 * F1


def toom_in(v):
    a, b = v[0] + v[2], v[1] + v[3]
    c, d = v[0] + 4.0 * v[2], 2.0 * v[1] + 8.0 * v[3]
    return [v[0], v[3], a + b, a - b, c + d, c - d]


def line_in(x):
    even, odd = x[0::2], x[1::2]
    both = [e + o for e, o in zip(even, odd)]
    return toom_in(both) + toom_in(odd) + toom_in(even)


def toom_kernel(k):
    h2, h1, h0 = k
    a, b = (h0 + h2) * 0.5, h1 * 0.5
    c, d = (h0 + 4.0 * h2) * (1.0 / 24.0), h1 * (1.0 / 12.0)
    return [h0, h2, a + b, a - b, c + d, c - d]


def line_kernel(t):
    k0 = [t[1], t[3], t[5]]
    up = [t[2] - t[1], t[4] - t[3], t[6] - t[5]]
    down = [t[0] - t[1], t[2] - t[3], t[4] - t[5]]
    return toom_kernel(k0) + toom_kernel(up) + toom_kernel(down)


def toom_out(m):
    z0, z5 = m[0], m[1]
    e1, o1 = m[2] + m[3], m[2] - m[3]
    e2, d2 = m[4] + m[5], m[4] - m[5]
    z4 = e2 - e1 * (1.0 / 3.0) + z0 * 0.25
    z2 = e1 - z0 - z4
    z3 = 2.0 * d2 - o1 * (1.0 / 3.0) - 5.0 * z5
    z1 = o1 - z3 - z5
    return [z1, z2, z3, z4]


def line_out(m):
    base, up, down = toom_out(m[0:6]), toom_out(m[6:12]), toom_out(m[12:18])
    out = []
    for i in range(4):
        out += [base[i] + up[i], base[i] + down[i]]
    return out


CHUNKS = 4


def all_signal(bb, count):
    barrier = pltpu.get_barrier_semaphore()

    def one(k, carry):
        pl.semaphore_signal(barrier, 1, device_id={"box": (bb + k) % count})
        return carry

    lax.fori_loop(1, count, one, 0)
    return barrier


def gather_kernel(
    child, interp, sel, angle, trans, out, tab_out,
    own, before, after, weights, weight, total, stage, cosine, sine, raw, tab_z, tab,
    load_sem, halo_send, halo_recv, move_send, move_recv, local_sem,
):
    bb, dd = lax.axis_index("box"), lax.axis_index("dir")
    boxes, dirs = lax.axis_size("box"), lax.axis_size("dir")
    rows = 2048 // CHUNKS
    barrier = all_signal(bb, boxes)
    above, below = (dd + 1) % dirs, (dd + dirs - 1) % dirs
    pl.semaphore_signal(barrier, 1, device_id={"dir": above})
    pl.semaphore_signal(barrier, 1, device_id={"dir": below})
    first = pl.multiple_of((bb // 2) * 128, 128)
    loads = [
        pltpu.make_async_copy(trans.at[:, :, pl.ds(first, 128)], raw, load_sem.at[0]),
        pltpu.make_async_copy(interp, weights, load_sem.at[1]),
        pltpu.make_async_copy(child, own, load_sem.at[2]),
    ]
    for copy in loads:
        copy.start()
    pl.semaphore_wait(barrier, boxes + 1)

    def halo(i):
        at = pl.ds(pl.multiple_of(i * rows, rows), rows)
        return [
            pltpu.make_async_remote_copy(
                child.at[at, pl.ds(256, 256)], before.at[at, :],
                halo_send.at[0, i], halo_recv.at[0, i], device_id={"dir": above},
            ),
            pltpu.make_async_remote_copy(
                child.at[at, pl.ds(0, 256)], after.at[at, :],
                halo_send.at[1, i], halo_recv.at[1, i], device_id={"dir": below},
            ),
        ]

    for i in range(CHUNKS):
        for copy in halo(i):
            copy.start()

    cosine[...] = jnp.cos(angle[...])
    sine[...] = jnp.sin(angle[...])
    loads[0].wait()
    for x in range(2, 5):
        for y in range(2, 5):
            for z in range(2, 5):
                raw[x * 49 + y * 7 + z] = jnp.zeros((2, 128), jnp.float32)

    def table_x(i, carry):
        t = [raw[x * 49 + i] for x in range(7)]
        vals = [t[1], t[3], t[5], t[2] - t[1], t[4] - t[3], t[6] - t[5]]
        vals += [t[0] - t[1], t[2] - t[3], t[4] - t[5]]
        for g, v in enumerate(vals):
            tab[i, g] = v
        return carry

    lax.fori_loop(0, 49, table_x, 0)

    def table_z(y, carry):
        def inner(g, carry):
            vals = line_kernel([tab[y * 7 + z, g] for z in range(7)])
            for fz, v in enumerate(vals):
                tab_z[y * F1 + fz, g] = v
            return carry

        return lax.fori_loop(0, 9, inner, carry)

    lax.fori_loop(0, 7, table_z, 0)

    def table_y(fz, carry):
        def inner(g, carry):
            vals = line_kernel([tab_z[y * F1 + fz, g] for y in range(7)])
            for fy, v in enumerate(vals):
                tab[fy * F1 + fz, g] = v
            return carry

        return lax.fori_loop(0, 9, inner, carry)

    lax.fori_loop(0, F1, table_y, 0)
    loads[1].wait()
    for j in range(16):
        for o in range(5):
            value = None
            for b in (o - 1, o):
                if 0 <= b < 4:
                    term = weights[j, b].astype(jnp.float32) * sel[(j * 5 + o) * 2 + (b == o)]
                    value = term if value is None else value + term
            lanes = pl.ds((j % 4) * 128, 128)
            weight[j // 4, pl.ds(o * 128, 128), lanes] = value.astype(jnp.bfloat16)
    keep = pltpu.make_async_copy(tab, tab_out, load_sem.at[3])
    keep.start()
    loads[2].wait()
    low = lax.broadcasted_iota(jnp.int32, (8, 128), 0) < 4

    def chunk(i, carry):
        for copy in halo(i):
            copy.wait_recv()
        at = pl.ds(pl.multiple_of(i * rows, rows), rows)
        for c in range(4):
            parts = []
            if c < 2:
                parts.append((before, c * 128, (2 - c) * 128, 0))
            lo, hi = max(c, 2), min(c + 5, 6)
            parts.append((own, (lo - 2) * 128, (hi - lo) * 128, (lo - c) * 128))
            if c > 1:
                parts.append((after, 0, (c - 1) * 128, (6 - c) * 128))
            acc = None
            for ref, col, width, wrow in parts:
                piece = jnp.dot(
                    ref[at, pl.ds(col, width)],
                    weight[c, pl.ds(wrow, width), :],
                    preferred_element_type=jnp.float32,
                )
                acc = piece if acc is None else acc + piece
            total[...] = acc

            def tile_of(tile, carry, c=c):
                lane = pl.multiple_of(tile * 128, 128)
                wide = pl.multiple_of(c * 512 + tile * 128, 128)
                for pair in range(rows // 256):
                    halves = [[], []]
                    for k in range(2):
                        re = im = None
                        for h in range(8):
                            base = (pair * 2 + k) * 128 + h * 16
                            ur = total[pl.ds(base, 8), pl.ds(lane, 128)]
                            ui = total[pl.ds(base + 8, 8), pl.ds(lane, 128)]
                            cs = jnp.broadcast_to(cosine[h : h + 1, pl.ds(wide, 128)], (8, 128))
                            sn = jnp.broadcast_to(sine[h : h + 1, pl.ds(wide, 128)], (8, 128))
                            r, m = cs * ur - sn * ui, sn * ur + cs * ui
                            re = r if re is None else re + r
                            im = m if im is None else im + m
                        halves[0].append(jnp.where(low, re, pltpu.roll(im, 4, 0)))
                        halves[1].append(jnp.where(low, pltpu.roll(re, 4, 0), im))
                    where = pl.ds(pl.multiple_of(i * (rows // 16) + pair * 16, 16), 16)
                    for k in range(2):
                        value = jnp.concatenate(halves[k], axis=0).astype(jnp.bfloat16)
                        stage[(c * 4 + tile) * 2 + k, where, :] = value
                return carry

            lax.fori_loop(0, 4, tile_of, 0)

        piece = pl.ds(pl.multiple_of(i * (rows // 16), rows // 16), rows // 16)

        def send(k, carry):
            peer = (bb + k) % boxes
            pltpu.make_async_remote_copy(
                stage.at[peer, piece, :], out.at[bb, piece, :], move_send, move_recv,
                device_id={"box": peer},
            ).start()
            return carry

        lax.fori_loop(1, boxes, send, 0)
        return carry

    lax.fori_loop(0, CHUNKS, chunk, 0)
    mine = pltpu.make_async_copy(stage.at[bb], out.at[bb], local_sem)
    mine.start()
    mine.wait()
    keep.wait()
    for i in range(CHUNKS):
        for copy in halo(i):
            copy.wait_send()
    most = pl.ds(0, boxes - 1)
    pltpu.make_async_copy(stage.at[most], stage.at[most], move_send).wait()
    pltpu.make_async_copy(out.at[most], out.at[most], move_recv).wait()


def gather(child, interp, sel, angle, trans):
    any_space = pl.BlockSpec(memory_space=pl.ANY)
    return pl.pallas_call(
        gather_kernel,
        in_specs=[
            any_space,
            any_space,
            pl.BlockSpec(memory_space=pltpu.SMEM),
            pl.BlockSpec(memory_space=pltpu.VMEM),
            any_space,
        ],
        out_specs=[any_space, any_space],
        out_shape=[
            jax.ShapeDtypeStruct((32, 128, 128), jnp.bfloat16),
            jax.ShapeDtypeStruct((NF, 9, 2, 128), jnp.float32),
        ],
        scratch_shapes=[
            pltpu.VMEM((2048, 512), jnp.bfloat16),
            pltpu.VMEM((2048, 256), jnp.bfloat16),
            pltpu.VMEM((2048, 256), jnp.bfloat16),
            pltpu.VMEM((16, 4, 128, 128), jnp.bfloat16),
            pltpu.VMEM((4, 640, 512), jnp.bfloat16),
            pltpu.VMEM((2048 // CHUNKS, 512), jnp.float32),
            pltpu.VMEM((32, 128, 128), jnp.bfloat16),
            pltpu.VMEM((8, 2048), jnp.float32),
            pltpu.VMEM((8, 2048), jnp.float32),
            pltpu.VMEM((343, 2, 128), jnp.float32),
            pltpu.VMEM((7 * F1, 9, 2, 128), jnp.float32),
            pltpu.VMEM((NF, 9, 2, 128), jnp.float32),
            pltpu.SemaphoreType.DMA((4,)),
            pltpu.SemaphoreType.DMA((2, CHUNKS)),
            pltpu.SemaphoreType.DMA((2, CHUNKS)),
            pltpu.SemaphoreType.DMA,
            pltpu.SemaphoreType.DMA,
            pltpu.SemaphoreType.DMA,
        ],
        compiler_params=pltpu.CompilerParams(collective_id=0, has_side_effects=True),
    )(child, interp, sel, angle, trans)


def translate_kernel(slot_parent, occupied, pats, table, out, grid_x, lines, spec, tab, sem):
    fetch = pltpu.make_async_copy(table, tab, sem)
    fetch.start()
    row = lax.broadcasted_iota(jnp.int32, (8, 128), 0)
    sign = jnp.where(row < 4, -1.0, 1.0).astype(jnp.float32)

    def place(i, carry):
        both = pats[pl.ds(pl.multiple_of(i * 16, 16), 16), :].astype(jnp.float32)
        for k in range(2):
            p = slot_parent[2 * i + k]
            grid_x[p] = both[8 * k : 8 * k + 8] * occupied[p]
        return carry

    lax.fori_loop(0, 256, place, 0, unroll=8)

    def in_z(i, carry):
        for f, v in enumerate(line_in([grid_x[i * 8 + z] for z in range(8)])):
            lines[i * F1 + f] = v
        return carry

    lax.fori_loop(0, 64, in_z, 0, unroll=4)

    def in_y(x, carry):
        def inner(fz, carry):
            vals = line_in([lines[(x * 8 + y) * F1 + fz] for y in range(8)])
            for fy, v in enumerate(vals):
                spec[fy * F1 + fz, x] = v
            return carry

        return lax.fori_loop(0, F1, inner, carry, unroll=3)

    lax.fori_loop(0, 8, in_y, 0)
    fetch.wait()

    def product(f, carry):
        src = [spec[f, q] for q in range(8)]
        turn = [sign * pltpu.roll(v, 4, 0) for v in src]
        sets = [
            ([src[2 * j] + src[2 * j + 1] for j in range(4)], [turn[2 * j] + turn[2 * j + 1] for j in range(4)]),
            (src[1::2], turn[1::2]),
            (src[0::2], turn[0::2]),
        ]
        sums = []
        for g, (x, t) in enumerate(sets):
            acc = [None] * 4
            for j in range(-1, 2):
                k = g * 3 + j + 1
                a = jnp.broadcast_to(tab[f, k, 0:1, :], (8, 128))
                b = jnp.broadcast_to(tab[f, k, 1:2, :], (8, 128))
                for i in range(4):
                    if 0 <= i + j < 4:
                        v = a * x[i + j] + b * t[i + j]
                        acc[i] = v if acc[i] is None else acc[i] + v
            sums.append(acc)
        for i in range(4):
            spec[f, 2 * i] = sums[0][i] + sums[1][i]
            spec[f, 2 * i + 1] = sums[0][i] + sums[2][i]
        return carry

    lax.fori_loop(0, NF, product, 0, unroll=2)

    def out_y(x, carry):
        def inner(fz, carry):
            vals = line_out([spec[fy * F1 + fz, x] for fy in range(F1)])
            for y, v in enumerate(vals):
                lines[(x * 8 + y) * F1 + fz] = v
            return carry

        return lax.fori_loop(0, F1, inner, carry, unroll=2)

    lax.fori_loop(0, 8, out_y, 0)

    def out_z(i, carry):
        for z, v in enumerate(line_out([lines[i * F1 + f] for f in range(F1)])):
            grid_x[i * 8 + z] = v
        return carry

    lax.fori_loop(0, 64, out_z, 0, unroll=2)

    def give(i, carry):
        vals = [grid_x[slot_parent[2 * i + k]] for k in range(2)]
        both = jnp.concatenate(vals, axis=0).astype(out.dtype)
        out[pl.ds(pl.multiple_of(i * 16, 16), 16), :] = both
        return carry

    lax.fori_loop(0, 256, give, 0, unroll=8)


def translate(pats, table, slot_parent, occupied):
    grid_spec = pltpu.PrefetchScalarGridSpec(
        num_scalar_prefetch=2,
        grid=(1,),
        in_specs=[
            pl.BlockSpec((4096, 128), lambda i, s, o: (0, 0)),
            pl.BlockSpec(memory_space=pl.ANY),
        ],
        out_specs=pl.BlockSpec((4096, 128), lambda i, s, o: (0, 0)),
        scratch_shapes=[
            pltpu.VMEM((512, 8, 128), jnp.float32),
            pltpu.VMEM((64 * F1, 8, 128), jnp.float32),
            pltpu.VMEM((NF, 8, 8, 128), jnp.float32),
            pltpu.VMEM((NF, 9, 2, 128), jnp.float32),
            pltpu.SemaphoreType.DMA,
        ],
    )
    return pl.pallas_call(
        translate_kernel,
        grid_spec=grid_spec,
        out_shape=jax.ShapeDtypeStruct((4096, 128), jnp.bfloat16),
    )(slot_parent, occupied, pats, table)


def return_kernel(src, out, send_sem, recv_sem, local_sem):
    bb = lax.axis_index("box")
    boxes = lax.axis_size("box")
    barrier = all_signal(bb, boxes)
    mine = pltpu.make_async_copy(src.at[bb], out.at[bb], local_sem)
    mine.start()
    pl.semaphore_wait(barrier, boxes - 1)

    def send(k, carry):
        peer = (bb + k) % boxes
        pltpu.make_async_remote_copy(
            src.at[peer], out.at[bb], send_sem, recv_sem, device_id={"box": peer}
        ).start()
        return carry

    lax.fori_loop(1, boxes, send, 0)
    mine.wait()
    most = pl.ds(0, boxes - 1)
    pltpu.make_async_copy(src.at[most], src.at[most], send_sem).wait()
    pltpu.make_async_copy(out.at[most], out.at[most], recv_sem).wait()


def give_back(src):
    any_space = pl.BlockSpec(memory_space=pl.ANY)
    return pl.pallas_call(
        return_kernel,
        in_specs=[any_space],
        out_specs=any_space,
        out_shape=jax.ShapeDtypeStruct(src.shape, src.dtype),
        scratch_shapes=[pltpu.SemaphoreType.DMA] * 3,
        compiler_params=pltpu.CompilerParams(collective_id=1, has_side_effects=True),
    )(src)


def arrange_kernel(got, out):
    low = lax.broadcasted_iota(jnp.int32, (8, 128), 0) < 4
    for pair in range(got.shape[1] // 16):
        for c in range(16):
            first = got[2 * c, pair * 16 : pair * 16 + 16, :].astype(jnp.float32)
            second = got[2 * c + 1, pair * 16 : pair * 16 + 16, :].astype(jnp.float32)
            for k in range(2):
                h0, h1 = first[8 * k : 8 * k + 8], second[8 * k : 8 * k + 8]
                s = pair * 2 + k
                out[s, 0, :, c * 128 : c * 128 + 128] = jnp.where(low, h0, pltpu.roll(h1, 4, 0))
                out[s, 1, :, c * 128 : c * 128 + 128] = jnp.where(low, pltpu.roll(h0, 4, 0), h1)


def arrange(got):
    return pl.pallas_call(
        arrange_kernel,
        grid=(4,),
        in_specs=[pl.BlockSpec((32, 32, 128), lambda i: (0, i, 0))],
        out_specs=pl.BlockSpec((4, 2, 8, 2048), lambda i: (i, 0, 0, 0)),
        out_shape=jax.ShapeDtypeStruct((16, 2, 8, 2048), jnp.float32),
    )(got)


def shards(child_pat, interp, interp_blocks, shift_angle, slot_parent, far_list, trans):
    centre = lax.axis_index("dir") * 4 + jnp.arange(16, dtype=jnp.int32)[:, None] // 4
    rel = (interp_blocks - centre + 2) % 16
    slots = jnp.arange(5, dtype=jnp.int32)[None, :, None]
    entry = jnp.clip(slots - 1 + jnp.arange(2, dtype=jnp.int32)[None, None, :], 0, 3)
    hit = jnp.sum((rel[:, None, None, :] == slots[..., None]) & (entry[..., None] == jnp.arange(4)), axis=3)
    sel = hit.astype(jnp.float32).reshape(160)
    pieces, table = gather(
        child_pat.reshape(2048, 512), interp, sel, shift_angle, jnp.transpose(trans, (1, 0, 2))
    )
    ident = jnp.arange(512, dtype=jnp.int32)[:, None]
    watch = jnp.concatenate([far_list[128:], far_list[256:384]], axis=0)
    occupied = jnp.any(watch == ident, axis=1).astype(jnp.float32)
    local = translate(pieces.reshape(4096, 128), table, slot_parent, occupied)
    return arrange(give_back(local.reshape(32, 128, 128)))


def solution(mesh):
    in_specs = (
        P("box", None, None, "dir"),
        P("dir", None, None, None),
        P("dir", None),
        P(None, "dir"),
        P(),
        P(),
        P(None, None, "dir"),
    )
    out_specs = P("box", None, None, "dir")
    return jax.shard_map(shards, mesh=mesh, in_specs=in_specs, out_specs=out_specs, check_vma=False)
```

time: 129 us -> 87.8 us (0.68)
  Pallas kernels: 48.9 us -> 81.9 us
  waiting for transfers between devices: 31.4 us -> 0 us
  blocking collectives: 21.4 us -> 0 us
  starting transfers between devices: 13.5 us -> 0 us
  local copies, waits for them, and re-layouts: 12.6 us -> 2.7 us
    pallas_call x1 -> x2, Pallas kernels: 21.8 us -> 61.8 us  [the longest x1 43.6 us: gather(): pl.pallas_call(gather_kernel, in_specs=[any_space, any_space, pl.BlockSpe...]
    ppermute x2 -> x0, waiting for transfers between devices: 23.5 us -> none  [the longest x1 20.2 us: shards(): after = lax.ppermute(flat[:, :256], 'dir', down)]
    all_to_all x1 -> x0, blocking collectives: 21.4 us -> none  [shards(): back = lax.all_to_all(local.reshape(32, 128, 128), 'box', 0, 0, tiled=True)]
    all_to_all x1 -> x0, starting transfers between devices: 9.88 us -> none  [shards(): pats = lax.all_to_all(pieces, 'box', 0, 0, tiled=True).reshape(4096, 128)]
    unnamed x9 -> x0, local copies, waits for them, and re-layouts: 9.28 us -> none
    all_to_all x1 -> x0, waiting for transfers between devices: 7.93 us -> none  [shards(): pats = lax.all_to_all(pieces, 'box', 0, 0, tiled=True).reshape(4096, 128)]
    pallas_call x1, Pallas kernels: 23.5 us -> 16.5 us  [translate(): pl.pallas_call(translate_kernel, grid_spec=grid_spec, out_shape=jax.Shape...]
    ppermute x2 -> x0, starting transfers between devices: 3.62 us -> none  [the longest x1 3.62 us: shards(): after = lax.ppermute(flat[:, :256], 'dir', down)]
  transfers between devices with their start and end apart: 3 -> 0, of which waited for: 3 -> 0; matrix products, arithmetic and copies ran while one was open for 8% -> 0% of each run, Pallas kernels for 0% -> 0%
where the time goes in v1:
time: 87.8 us; the launch traced here: 86.3 us
  Pallas kernels  81.9 us (93%)
  local copies, waits for them, and re-layouts  2.7 us (3%)
  other arithmetic  1.62 us (2%)
    pallas_call x1, Pallas kernels, gather(): pl.pallas_call(gather_kernel, in_specs=[any_space, any_space, pl.BlockSpe...  43.6 us
    pallas_call x1, Pallas kernels, give_back(): pl.pallas_call(return_kernel, in_specs=[any_space], out_specs=any_space,...  18.2 us
    pallas_call x1, Pallas kernels, translate(): pl.pallas_call(translate_kernel, grid_spec=grid_spec, out_shape=jax.Shape...  16.5 us
    pallas_call x1, Pallas kernels, arrange(): pl.pallas_call(arrange_kernel, grid=(4,), in_specs=[pl.BlockSpec((32, 32,...  3.63 us
    slice x2, local copies, waits for them, and re-layouts, shards(): watch = jnp.concatenate([far_list[128:], far_list[256:384]], axis=0)  1.88 us

profile of v1, /device:TPU:1, one launch (start us, length us, event | category | flops | bytes accessed | tf_op | source)
XLA Modules:
  0.0 86.3 jit_solution(6071531471396001650)
XLA Ops:
  0.0 0.7 add_select_fusion
  0.7 0.1 add_clamp_fusion
  0.8 0.1 iota_compare_fusion.1
  0.9 0.1 convert_reduce_fusion
  1.0 0.1 copy.10
  1.1 0.7 convert_element_type.16.sel
  1.8 0.9 %slice.7 = s32[128,189]{0,1:T(8,128)S(1)} slice(s32[512,189]{0,1:T(8,128)} %param.12), slice={[256:384], [0:189]} | slice | bytes 193536 | tf_op jit(solution)/shard_map/slice | solution.py:459
  2.7 1.0 %slice.6 = s32[384,189]{0,1:T(8,128)S(1)} slice(s32[512,189]{0,1:T(8,128)} %param.12), slice={[128:512], [0:189]} | slice | bytes 580608 | tf_op jit(solution)/shard_map/slice | solution.py:459
  3.7 0.1 fusion
  3.8 0.6 convert_element_type.13.occupied
  4.3 43.6 %shard_map.73 = (bf16[32,128,128]{2,1,0:T(8,128)(2,1)}, f32[324,9,2,128]{3,2,1,0:T(2,128)}) custom-call(bf16[2048,512]{1,0:T(8,128)(2,1)} %bitcast.6, bf16[16,4,128,128]{3,2,1,0:T(8,128)(2,1)} %interp.1, f32[160]{0:T(256)} %convert_element_type.16.sel, f32[8,2048]{1,0:T(8,128)} %angle.1, f32[343,2,2048]{2,1,0:T(2,128)} %bitcast.4), custom_call_target="tpu_custom_call" | custom-call | tf_op jit(solution)/shard_map/pallas_call | solution.py:241
  47.9 16.5 %shard_map.74 = bf16[4096,128]{1,0:T(8,128)(2,1)} custom-call(s32[512]{0:T(512)} %slot_parent.1, f32[512]{0:T(512)} %convert_element_type.13.occupied, bf16[4096,128]{1,0:T(8,128)(2,1)} %bitcast.7, f32[324,9,2,128]{3,2,1,0:T(2,128)} %get-tuple-element.8.table), custom_call_target="tpu_custom_call" | custom-call | tf_op jit(solution)/shard_map/pallas_call | solution.py:384
  64.4 18.2 %shard_map.75.got = bf16[32,128,128]{2,1,0:T(8,128)(2,1)} custom-call(bf16[32,128,128]{2,1,0:T(8,128)(2,1)} %bitcast.5), custom_call_target="tpu_custom_call" | custom-call | tf_op jit(solution)/shard_map/pallas_call | solution.py:415
  82.6 3.6 %shard_map.76 = f32[16,2,8,2048]{3,2,1,0:T(8,128)} custom-call(bf16[32,128,128]{2,1,0:T(8,128)(2,1)} %shard_map.75.got), custom_call_target="tpu_custom_call" | custom-call | tf_op jit(solution)/shard_map/pallas_call | solution.py:439
  (4 shorter events, 0.0 us)
